TPU v7x, 768 devices: a whole 4x8x12 slice. The times are simulated.
768 devices in a mesh: grp: 48 (over x, z_lo, core), col: 8 (over y), dev: 2 (over z_hi).
Axes of the slice: x: 4, y: 8, z: 12 (z_hi: 2, z_lo: 6; z = z_hi * 6 + z_lo), core: 2. Of those that a mesh axis runs over, the one named last changes fastest.
Arguments:
- rho_re: float32 [12288, 512], P(('grp', 'col'), 'dev'), may hold values from -0.078125 to 0.078125
- rho_im: float32 [12288, 512], P(('grp', 'col'), 'dev'), may hold values from -0.078125 to 0.078125
- coulomb: float32 [12288], P(('grp', 'col', 'dev')), may hold values from 0.4 to 1.6
- chi_prev: float32 [2, 48, 8, 32, 12288], P(None, None, 'col', 'dev', 'grp'), may hold values from -0.013671875 to 0.013671875
- source: float32 [12288, 128], P(('grp', 'col', 'dev')), may hold values from -6 to 6
- band_v: int32 [512], P('dev'), may hold values from 0 to 127
- band_c: int32 [512], P('dev'), may hold values from 128 to 255
- band_energy: float32 [256], replicated, may hold values from -2 to 2.5, as said below
- band_occ: float32 [256], replicated, may hold values from 0 to 1, as said below
Outputs:
- screened_re: float32 [12288, 128], P(('grp', 'col', 'dev'))
- screened_im: float32 [12288, 128], P(('grp', 'col', 'dev'))
Inputs may be any that keep to these rules, and one draw needn't show every extreme that they name: `band_v`: the valence bands are the first 128. `band_energy`: the first 128 bands lie below -0.1, the others above 0.2. `band_occ`: the first 128 bands have occupations of 0.7 or more, the others of 0.3 or less.
All inputs are finite; a program needn't handle non-finite values.
Results may differ from a plain program's by a relative error of at most 0.00013.
Values sent between devices are 32-bit elements; how exact they have to be, the bound alone decides.
A program may use at most 32 MiB of HBM per device.

v0:
```python
import jax
import jax.numpy as jnp
from jax import lax
from jax.sharding import PartitionSpec as P

ITERS = 2


frequency = 0.8
damping = 0.5


def contract(left, right):
    return lax.dot_general(
        left,
        right,
        (((0,), (0,)), ((), ())),
        precision=lax.Precision.HIGHEST,
        preferred_element_type=jnp.float32,
    )


def contract_last(left, right):
    return lax.dot_general(
        left,
        right,
        (((1,), (1,)), ((), ())),
        precision=lax.Precision.HIGHEST,
        preferred_element_type=jnp.float32,
    )


def lookup(bands, table):
    band_index = jnp.arange(table.shape[0], dtype=jnp.int32)
    match = bands[:, None] == band_index[None, :]
    return jnp.sum(jnp.where(match, table[None, :], 0.0), axis=1)


def shards(rho_re, rho_im, coulomb, chi_prev, source, band_v, band_c, band_energy, band_occ):
    delta = lookup(band_c, band_energy) - lookup(band_v, band_energy)
    filling = lookup(band_v, band_occ) - lookup(band_c, band_occ)
    weight = filling * 2.0 * delta / (delta * delta + frequency * frequency)
    half_pairs = rho_re.shape[1]
    width = source.shape[1]
    row_block = chi_prev.shape[4]
    my_cols = chi_prev.shape[1] * chi_prev.shape[3]
    previous = chi_prev.reshape(2, my_cols, row_block)
    halves = lax.axis_size("dev")
    stacked = jnp.stack([rho_re, rho_im], axis=1)
    weight_rows = jnp.broadcast_to(weight[None, None, :], (halves, 1, half_pairs))
    mine_pairs, all_weight = (
        lax.all_to_all(stacked, "dev", split_axis=0, concat_axis=2, tiled=True),
        lax.all_to_all(weight_rows, "dev", split_axis=0, concat_axis=2, tiled=True),
    )
    all_pairs = mine_pairs.shape[2]
    pair_weights = all_weight.reshape(all_pairs)
    row_pairs = lax.all_gather(mine_pairs, ("col", "dev"), axis=0, tiled=True)
    rows_re = row_pairs[:, 0, :] * pair_weights[None, :]
    rows_im = row_pairs[:, 1, :] * pair_weights[None, :]
    left_re = jnp.concatenate([rows_re, rows_im], axis=1)
    left_im = jnp.concatenate([rows_im, -rows_re], axis=1)
    piece = lax.all_gather(mine_pairs, "grp", axis=0, tiled=True)
    flat = piece.reshape(piece.shape[0], 2 * all_pairs)
    part_re = -contract_last(flat, left_re)
    part_im = -contract_last(flat, left_im)
    fresh = jnp.concatenate([part_re, part_im], axis=1)
    tile_re = previous[0] + fresh[:, :row_block]
    tile_im = previous[1] + fresh[:, row_block:]
    scale = coulomb[:, None]
    real_part = source
    imag_part = jnp.zeros_like(source)
    for sweep in range(ITERS):
        scaled = jnp.concatenate([scale * real_part, scale * imag_part], axis=1)
        accumulate_piece = lax.all_gather(scaled, "grp", axis=0, tiled=True)
        swapped = jnp.concatenate(
            [-accumulate_piece[:, width:], accumulate_piece[:, :width]], axis=1
        )
        total = contract(tile_re, accumulate_piece) + contract(tile_im, swapped)
        mine = lax.psum_scatter(total, ("col", "dev"), scatter_dimension=0, tiled=True)
        image_re = scale * mine[:, :width]
        image_im = scale * mine[:, width:]
        real_part = real_part + damping * (source + image_re - real_part)
        imag_part = imag_part + damping * (image_im - imag_part)
    return (real_part, imag_part)


def solution(mesh):
    placed = (
        P(("grp", "col"), "dev"),
        P(("grp", "col"), "dev"),
        P(("grp", "col", "dev")),
        P(None, None, "col", "dev", "grp"),
        P(("grp", "col", "dev"), None),
        P("dev"),
        P("dev"),
        P(),
        P(),
    )
    return jax.shard_map(
        shards,
        mesh=mesh,
        in_specs=placed,
        out_specs=(P(("grp", "col", "dev"), None), P(("grp", "col", "dev"), None)),
        check_vma=False,
    )
```

profile of v0, /device:TPU:1, one launch (start us, length us, event | category | flops | bytes accessed | tf_op | source)
XLA Modules:
  0.0 809.8 jit_solution(9751970532722324555)
XLA Ops:
  7.2 0.0 all-gather.5.cloned.1.call-start
  7.2 0.8 stack.10
  8.0 0.8 stack.9
  8.8 0.1 pad_maximum_fusion
  8.9 24.9 %all_to_all.27 = f32[32,2,256]{2,1,0:T(2,128)S(1)} all-to-all(f32[32,2,256]{2,1,0:T(2,128)S(1)} %pad_maximum_fusion), channel_id=1, replica_groups=mesh['grp'=48,'col'=8,'dev'=2] {'dev'}, dimensions={0} | all-to-all | bytes 131072 | tf_op jit(solution)/shard_map/all_to_all | solution.py:52
  33.8 0.1 copy.20
  33.8 0.7 all_to_all.23
  34.5 0.0 all-gather.5.cloned.1.call-update
  34.5 0.0 all-gather.3.cloned.1.call-start
  34.6 0.7 all-gather.3.cloned.1.call-update
  35.3 1.1 select_reduce_fusion.2
  36.3 0.6 broadcast_in_dim.51
  36.9 3.2 all-to-all-start.1
  40.2 0.0 reduce-scatter.3.cloned.1.call-start
  40.2 0.7 broadcast_multiply_fusion.1
  40.9 0.8 broadcast_multiply_fusion
  41.6 0.1 mul.122
  41.7 2.7 fusion.33
  44.4 88.4 %all_gather.14 = f32[768,256]{1,0:T(8,128)S(1)} all-gather(f32[16,256]{1,0:T(8,128)S(1)} %pad_maximum_fusion.1), channel_id=1, replica_groups=mesh['grp'=48,'col'=8,'dev'=2] {'grp'}, dimensions={0}, use_global_device_ids=true | all-gather | bytes 802816 | tf_op jit(solution)/shard_map/all_gather | solution.py:74
  132.8 0.9 copy-done
  133.7 0.8 slice_negate_fusion.1
  134.6 0.0 all-to-all-done.1
  134.6 3.0 all-gather.5.cloned.1.call-done
  137.6 2.5 fusion.31
  140.1 94.1 %all-gather.3.cloned.1.call-done = f32[768,2,512]{2,0,1:T(8,128)} async-done(((f32[16,2,512]{2,0,1:T(8,128)}), f32[768,2,512]{2,0,1:T(8,128)}) %all-gather.3.cloned.1.call-update) | async-done | bytes 3145744 | tf_op jit(solution)/shard_map/all_gather | solution.py:62
  234.2 2.6 copy.18
  236.8 6.7 fusion.1
  243.5 1.5 fusion.34
  244.9 0.0 copy-start.9
  244.9 0.0 copy-done.6
  244.9 0.0 copy-done.7
  244.9 0.0 copy-done.8
  245.0 0.0 copy-start.10
  245.0 0.0 copy-start.12
  245.0 5.1 fusion
  250.1 0.9 copy-done.4
  251.0 2.4 convolution_add_fusion.1
  253.4 0.0 reduce-scatter.3.cloned.1.call-update
  253.4 0.0 reduce-scatter.5.cloned.1.call-start
  253.4 230.3 %reduce-scatter.3.cloned.1.call-done = f32[16,256]{1,0:T(8,128)} async-done(((f32[256,256]{1,0:T(8,128)}), f32[16,256]{1,0:T(8,128)}) %reduce-scatter.3.cloned.1.call-update) | async-done | bytes 16400 | tf_op jit(solution)/shard_map/reduce_scatter | solution.py:79
  483.8 0.8 fusion.26
  484.6 86.2 %all_gather.15 = f32[768,256]{1,0:T(8,128)S(1)} all-gather(f32[16,256]{1,0:T(8,128)S(1)} %pad_maximum_fusion.2), channel_id=1, replica_groups=mesh['grp'=48,'col'=8,'dev'=2] {'grp'}, dimensions={0}, use_global_device_ids=true | all-gather | bytes 802816 | tf_op jit(solution)/shard_map/all_gather | solution.py:74
  570.8 0.1 slice_negate_fusion
  570.8 1.4 fusion.35
  572.3 2.1 convolution_add_fusion
  574.4 0.0 reduce-scatter.5.cloned.1.call-update
  574.4 227.5 %reduce-scatter.5.cloned.1.call-done = f32[16,256]{1,0:T(8,128)} async-done(((f32[256,256]{1,0:T(8,128)}), f32[16,256]{1,0:T(8,128)}) %reduce-scatter.5.cloned.1.call-update) | async-done | bytes 16400 | tf_op jit(solution)/shard_map/reduce_scatter | solution.py:79
  801.9 1.4 fusion.20
  (21 shorter events, 0.1 us)
Async XLA Ops:
  7.2 130.5 %all-gather.5.cloned.1.call-start = ((), (), s32[]{:S(2)}) async-start(), calls=%async_computation.5 | async-start | bytes 1114112 | tf_op jit(solution)/shard_map/all_gather | solution.py:57
  34.5 199.6 %all-gather.3.cloned.1.call-start = ((), (), s32[]{:S(2)}) async-start(), calls=%async_computation.4 | async-start | bytes 3211264 | tf_op jit(solution)/shard_map/all_gather | solution.py:62
  36.9 97.7 %all-to-all-start.1 = ((f32[2,1,256]{2,1,0:T(1,128)}), f32[2,1,256]{2,1,0:T(1,128)S(1)}, u32[]{:S(2)}, u32[]{:S(2)}) async-start(f32[2,1,256]{2,1,0:T(1,128)} %broadcast_in_dim.51), calls=%async_computation.1 | async-start | bytes 4096 | tf_op jit(solution)/shard_map/all_to_all | solution.py:53
  40.2 443.6 %reduce-scatter.3.cloned.1.call-start = ((), (), s32[]{:S(2)}) async-start(), calls=%async_computation.6 | async-start | bytes 278528 | tf_op jit(solution)/shard_map/reduce_scatter | solution.py:79
  132.8 0.9 copy-start
  236.7 6.7 copy-start.1
  236.7 8.2 %copy-start.6 = (f32[256,512]{1,0:T(8,128)S(1)}, f32[256,512]{1,0:T(8,128)}, u32[]{:S(2)}) copy-start(f32[256,512]{1,0:T(8,128)} %get-tuple-element.10) | copy-start | bytes 1572868
  236.7 8.2 %copy-start.7 = (f32[1,48,1,16,256]{4,3,2,1,0:T(8,128)S(1)}, f32[1,48,1,16,256]{4,3,2,1,0:T(8,128)}, u32[]{:S(2)}) copy-start(f32[1,48,1,16,256]{4,3,2,1,0:T(8,128)} %get-tuple-element.8) | copy-start | bytes 2359300
  236.8 8.2 %copy-start.8 = (f32[256,512]{1,0:T(8,128)S(1)}, f32[256,512]{1,0:T(8,128)}, u32[]{:S(2)}) copy-start(f32[256,512]{1,0:T(8,128)} %get-tuple-element.6) | copy-start | bytes 1572868
  243.4 6.6 copy-start.2
  244.9 6.1 copy-start.9
  245.0 238.8 %copy-start.10 = (f32[16,128]{1,0:T(8,128)S(1)}, f32[16,128]{1,0:T(8,128)}, u32[]{:S(2)}) copy-start(f32[16,128]{1,0:T(8,128)} %param.13) | copy-start | bytes 24580
  245.0 238.8 %copy-start.12 = (f32[16]{0:T(128)S(1)}, f32[16]{0:T(128)}, u32[]{:S(2)}) copy-start(f32[16]{0:T(128)} %param.11) | copy-start | bytes 196
  250.1 0.9 copy-start.4
  250.1 320.7 %copy-start.3 = (f32[768,256]{1,0:T(8,128)S(1)}, f32[768,256]{1,0:T(8,128)}, u32[]{:S(2)}) copy-start(f32[768,256]{1,0:T(8,128)} %copy-done.2) | copy-start | bytes 2359300
  253.4 318.9 %copy-start.5 = (f32[768,256]{1,0:T(8,128)S(1)}, f32[768,256]{1,0:T(8,128)}, u32[]{:S(2)}) copy-start(f32[768,256]{1,0:T(8,128)} %copy-done.4) | copy-start | bytes 2359300
  253.4 548.5 %reduce-scatter.5.cloned.1.call-start = ((), (), s32[]{:S(2)}) async-start(), calls=%async_computation.7 | async-start | bytes 278528 | tf_op jit(solution)/shard_map/reduce_scatter | solution.py:79
  484.6 317.3 %copy-start.11 = (f32[16,256]{1,0:T(8,128)S(1)}, f32[16,256]{1,0:T(8,128)}, u32[]{:S(2)}) copy-start(f32[16,256]{1,0:T(8,128)} %reduce-scatter.3.cloned.1.call-done) | copy-start | bytes 49156
Sparse Core Ops, SparseCore 0:
  34.6 102.9 all-gather.4
  140.0 94.0 all-gather.2
  253.5 230.2 reduce-scatter.2
  574.5 227.2 reduce-scatter.4
where the time goes:
time: 815 us; the launch traced here: 810 us
  waiting for transfers between devices  556 us (68%)
  blocking collectives  200 us (25%)
  matrix products  19.1 us (2%)
  between operations  14 us (2%)
  local copies, waits for them, and re-layouts  10 us (1%)
    reduce_scatter x2, waiting for transfers between devices, shards(): lax.psum_scatter(total, ('col', 'dev'), scatter_dimension=0, tiled=True)  458 us
    all_gather x2, blocking collectives, shards(): accumulate_piece = lax.all_gather(scaled, 'grp', axis=0, tiled=True)  175 us
    all_gather x1, waiting for transfers between devices, shards(): piece = lax.all_gather(mine_pairs, 'grp', axis=0, tiled=True)  94.1 us
    all_to_all x1, blocking collectives, shards(): lax.all_to_all(stacked, 'dev', split_axis=0, concat_axis=2, tiled=True)  24.9 us
  transfers between devices with their start and end apart: 5, of which 4 were waited for; matrix products, arithmetic and copies ran while one was open for 1% of the time, Pallas kernels for 0%

commit v1 on v0

v1 whole, which is shorter than its diff:
```python
import functools

import jax
import jax.numpy as jnp
from jax import lax
from jax.experimental import pallas as pl
from jax.experimental.pallas import tpu as pltpu
from jax.sharding import PartitionSpec as P

ITERS = 2
NX = 4
NZ = 6
NC = 2
W = 128
frequency = 0.8
damping = 0.5
F32 = jnp.float32
BF16 = jnp.bfloat16
MESH = pl.DeviceIdType.MESH


def split(value):
    high = value.astype(BF16)
    low = (value - high.astype(F32)).astype(BF16)
    return high, low


def dot(left, right):
    return jnp.dot(left, right, preferred_element_type=F32)


def column(row):
    n = row.shape[1]
    down = lax.broadcasted_iota(jnp.int32, (n, n), 0)
    across = lax.broadcasted_iota(jnp.int32, (n, n), 1)
    return jnp.sum(jnp.where(down == across, row, 0.0), axis=1, keepdims=True)


def kernel(ny, rho_re, rho_im, coulomb, chi_prev, source, band_v, band_c, energy, occ,
           out_re, out_im,
           tile, wide_hi, wide_lo, pairs_t, pairs_w_hi, pairs_w_lo, both, grid1, grid2,
           part0, sib_in, part1, x_in, part2, y_in, z_all, full, sums, sums_in, halves, scaled, state, last, last_in,
           tile_sem, both_sem, gz_send, gx_send, gs_send, g_recv, gs_recv,
           sib_sem, xr_send, xr_recv, yr_send, yr_recv, za_send, za_recv, yg_send, yg_recv,
           xg_send, xg_recv, sg_send, sg_recv, rs_send, rs_recv, h_sem):
    grp = lax.axis_index("grp")
    my_y = lax.axis_index("col")
    my_k = lax.axis_index("dev")
    my_c = lax.rem(grp, NC)
    my_z = lax.rem(lax.div(grp, NC), NZ)
    my_x = lax.div(grp, NC * NZ)
    other_c = 1 - my_c
    other_k = 1 - my_k
    groups = NX * NZ * NC
    n_pairs = rho_re.shape[1]
    n_tiles = full.shape[3]
    per_y = n_tiles // ny
    block = tile.shape[4]

    def at(x=None, y=None, z=None, c=None, k=None):
        x = my_x if x is None else x
        y = my_y if y is None else y
        z = my_z if z is None else z
        c = my_c if c is None else c
        k = my_k if k is None else k
        return ((x * NZ + z) * NC + c, y, k)

    x_peers = [lax.rem(my_x + d, NX) for d in range(1, NX)]
    y_peers = [lax.rem(my_y + d, ny) for d in range(1, ny)]
    z_peers = [lax.rem(my_z + d, NZ) for d in range(1, NZ)]
    everyone = (
        [at(x=x) for x in x_peers]
        + [at(y=y) for y in y_peers]
        + [at(z=z) for z in z_peers]
        + [at(c=other_c), at(k=other_k)]
    )

    def remote(src, dst, send, recv, device):
        return pltpu.make_async_remote_copy(
            src_ref=src, dst_ref=dst, send_sem=send, recv_sem=recv, device_id=device, device_id_type=MESH
        )

    sent = []

    def send(src, dst, s, r, device):
        copy = remote(src, dst, s, r, device)
        copy.start()
        sent.append(copy)

    def arrive(dst, s, r):
        remote(dst, dst, s, r, at(c=other_c)).wait_recv()

    load = pltpu.make_async_copy(chi_prev, tile, tile_sem)
    load.start()

    scale16 = column(coulomb[...])
    src16 = source[...]
    both[my_k] = jnp.concatenate([src16, jnp.broadcast_to(scale16, (16, W))], axis=1)
    grid1[my_c, my_x, my_z] = scale16 * src16

    barrier = pltpu.get_barrier_semaphore()
    for device in everyone:
        pl.semaphore_signal(barrier, inc=1, device_id=device, device_id_type=MESH)
    pl.semaphore_wait(barrier, len(everyone))

    send(both.at[my_k], both.at[my_k], both_sem.at[0], both_sem.at[1], at(k=other_k))

    def gather_start(grid, i):
        own = grid.at[my_c, my_x, my_z]
        for j, z in enumerate(z_peers):
            send(own, own, gz_send.at[i, j], g_recv.at[i, my_x, my_z], at(z=z))
        for j, x in enumerate(x_peers):
            send(own, own, gx_send.at[i, j, my_z], g_recv.at[i, my_x, my_z], at(x=x))

    def gather_z(grid, i):
        def relay(z):
            held = grid.at[my_c, my_x, z]
            arrive(held, gz_send.at[i, 0], g_recv.at[i, my_x, z])
            for j, x in enumerate(x_peers):
                remote(held, held, gx_send.at[i, j, z], g_recv.at[i, my_x, z], at(x=x)).start()

        for d in range(1, NZ):
            @pl.when(my_z + d < NZ)
            def _():
                relay(my_z + d)

            @pl.when(my_z - d >= 0)
            def _():
                relay(my_z - d)

        row = grid.at[my_c, my_x]
        send(row, row, gs_send.at[i, my_x], gs_recv.at[i, my_x], at(c=other_c))

    def gather_x(grid, i):
        for j in (0, NX - 2, 1) if NX == 4 else range(NX - 1):
            x = x_peers[j]
            for z in range(NZ):
                arrive(grid.at[my_c, x, z], gz_send.at[i, 0], g_recv.at[i, x, z])
            row = grid.at[my_c, x]
            send(row, row, gs_send.at[i, x], gs_recv.at[i, x], at(c=other_c))

    def gather_end(grid, i):
        for x in range(NX):
            arrive(grid.at[other_c, x], gs_send.at[i, 0], gs_recv.at[i, x])
        value = jnp.concatenate(
            [grid[c, x, z] for x in range(NX) for z in range(NZ) for c in range(NC)], axis=0
        )
        return split(value)

    def gather_close(grid, i):
        for j, x in enumerate(x_peers):
            for d in range(1, NZ):
                z = z_peers[d - 1]
                held = grid.at[my_c, my_x, z]
                remote(held, held, gx_send.at[i, j, z], g_recv.at[i, my_x, z], at(x=x)).wait_send()

    def project(v_re, v_im, i):
        stacked = jnp.concatenate(
            [jnp.concatenate([v_re, v_im], axis=1), jnp.concatenate([v_im, -v_re], axis=1)], axis=0
        )
        high, low = split(stacked)
        value = dot(pairs_t[...], jnp.concatenate([high, high, low], axis=0))
        count = n_pairs // NC // NX
        for c in range(NC):
            for x in range(NX):
                for t in range(n_tiles):
                    row = (c * NX + x) * count + (t // 2) * 8
                    lane = (t % 2) * W
                    part0[i, c, x, t] = value[row : row + 8, lane : lane + W]
        send(part0.at[i, other_c], sib_in.at[i], sib_sem.at[0, i], sib_sem.at[1, i], at(c=other_c))

    def reduce_x(i):
        arrive(sib_in.at[i], sib_sem.at[0, i], sib_sem.at[1, i])
        part1[i] = part0[i, my_c] + sib_in[i]
        for j, x in enumerate(x_peers):
            send(part1.at[i, x], x_in.at[i, my_x], xr_send.at[i, j], xr_recv.at[i, my_x], at(x=x))

    def reduce_y(i):
        total = part1[i, my_x]
        for x in x_peers:
            arrive(x_in.at[i, x], xr_send.at[i, 0], xr_recv.at[i, x])
            total = total + x_in[i, x]
        part2[i] = total.reshape(part2.shape[1:])
        for j, y in enumerate(y_peers):
            send(part2.at[i, y], y_in.at[i, my_y], yr_send.at[i, j], yr_recv.at[i, my_y], at(y=y))

    def reduce_z(i):
        total = part2[i, my_y]
        for y in y_peers:
            arrive(y_in.at[i, y], yr_send.at[i, 0], yr_recv.at[i, y])
            total = total + y_in[i, y]
        z_all[i, my_z] = total
        for j, z in enumerate(z_peers):
            send(z_all.at[i, my_z], z_all.at[i, my_z], za_send.at[i, j], za_recv.at[i, my_z], at(z=z))

    def spread_y(i):
        for z in z_peers:
            arrive(z_all.at[i, z], za_send.at[i, 0], za_recv.at[i, z])
        total = z_all[i, 0]
        for z in range(1, NZ):
            total = total + z_all[i, z]
        mine = pl.ds(my_y * per_y, per_y)
        full[i, my_c, my_x, mine] = total
        own = full.at[i, my_c, my_x, mine]
        for j, y in enumerate(y_peers):
            send(own, own, yg_send.at[i, j], yg_recv.at[i, my_y], at(y=y))

    def spread_x(i):
        for y in y_peers:
            arrive(full.at[i, my_c, my_x, pl.ds(y * per_y, per_y)], yg_send.at[i, 0], yg_recv.at[i, y])
        own = full.at[i, my_c, my_x]
        for j, x in enumerate(x_peers):
            send(own, own, xg_send.at[i, j], xg_recv.at[i, my_x], at(x=x))
        send(own, own, sg_send.at[i, my_x], sg_recv.at[i, my_x], at(c=other_c))

    def spread_core(i):
        for x in x_peers:
            held = full.at[i, my_c, x]
            arrive(held, xg_send.at[i, 0], xg_recv.at[i, x])
            send(held, held, sg_send.at[i, x], sg_recv.at[i, x], at(c=other_c))

    def expand(i):
        for x in range(NX):
            arrive(full.at[i, other_c, x], sg_send.at[i, 0], sg_recv.at[i, x])
        lanes = []
        for lane in range(2):
            lanes.append(jnp.concatenate(
                [full[i, c, x, t] for c in range(NC) for x in range(NX) for t in range(lane, n_tiles, 2)], axis=0
            ))
        high, low = split(jnp.concatenate(lanes, axis=1))
        left = pairs_w_hi[...]
        value = dot(left, high) + dot(left, low) + dot(pairs_w_lo[...], high)
        return value[:32, :W] - value[32:, W:], value[:32, W:] + value[32:, :W]

    def scatter_start(re, im, i):
        for y in range(ny):
            sums[i, y] = jnp.concatenate([re[y * 32 : y * 32 + 32], im[y * 32 : y * 32 + 32]], axis=1)
        for j, y in enumerate(y_peers):
            send(sums.at[i, y], sums_in.at[i, my_y], rs_send.at[i, j], rs_recv.at[i, my_y], at(y=y))

    def scatter_end(i):
        total = sums[i, my_y]
        for y in y_peers:
            arrive(sums_in.at[i, y], rs_send.at[i, 0], rs_recv.at[i, y])
            total = total + sums_in[i, y]
        return total

    gather_start(grid1, 0)

    down = lax.broadcasted_iota(jnp.int32, (energy.shape[1], n_pairs), 0)
    in_v = down == band_v[...]
    in_c = down == band_c[...]
    e_col = column(energy[...])
    o_col = column(occ[...])

    def pick(match, table):
        return jnp.sum(jnp.where(match, table, 0.0), axis=0, keepdims=True)

    delta = pick(in_c, e_col) - pick(in_v, e_col)
    filling = pick(in_v, o_col) - pick(in_c, o_col)
    weight = filling * 2.0 * delta / (delta * delta + frequency * frequency)
    stacked_pairs = jnp.concatenate([rho_re[...], rho_im[...]], axis=0)
    high, low = split(stacked_pairs)
    high, low = high.astype(F32), low.astype(F32)
    pairs_t[...] = jnp.concatenate([high, low, high], axis=0).T.astype(BF16)
    high, low = split(stacked_pairs * weight)
    pairs_w_hi[...] = high
    pairs_w_lo[...] = low

    load.wait()
    for part in range(2):
        for step in range(groups // 8):
            turned = tile[part, step * 8 : step * 8 + 8, 0].reshape(128, block).T
            high, low = split(turned)
            rows = pl.ds(part * block, block)
            lanes = pl.ds(step * 128, 128)
            wide_hi[rows, lanes] = high
            wide_lo[rows, lanes] = low

    arrive(both.at[other_k], both_sem.at[0], both_sem.at[1])
    held = both[...].reshape(32, 2 * W)
    src = held[:, :W]
    scale = held[:, W:]
    real_part = src
    imag_part = jnp.zeros_like(src)

    for i in range(ITERS):
        grid = grid1 if i == 0 else grid2
        v_re = scale * real_part
        v_im = scale * imag_part
        if i > 0:
            scaled[...] = jnp.concatenate([v_re, v_im], axis=1).reshape(scaled.shape)
            grid[my_c, my_x, my_z] = scaled[my_k]
            gather_start(grid, i)
        project(v_re, v_im, i)
        gather_z(grid, i)
        reduce_x(i)
        reduce_y(i)
        gather_x(grid, i)
        reduce_z(i)
        high, low = gather_end(grid, i)
        if i == 0:
            value = dot(wide_hi[...], jnp.concatenate([high, low], axis=1))
            value = value[:, :W] + value[:, W:] + dot(wide_lo[...], high)
            scatter_start(value[:block], value[block:], i)
        else:
            value = dot(wide_hi[...], high) + dot(wide_hi[...], low) + dot(wide_lo[...], high)
            scatter_start(value[:block, :W] - value[block:, W:], value[:block, W:] + value[block:, :W], i)
        spread_y(i)
        spread_x(i)
        total = scatter_end(i)
        spread_core(i)
        q_re, q_im = expand(i)
        total = total - jnp.concatenate([q_re, q_im], axis=1)
        if i < ITERS - 1:
            halves[my_k] = total
            send(halves.at[my_k], halves.at[my_k], h_sem.at[0, i], h_sem.at[1, i], at(k=other_k))
            arrive(halves.at[other_k], h_sem.at[0, i], h_sem.at[1, i])
            image = halves[0] + halves[1]
            image_re = scale * image[:, :W]
            image_im = scale * image[:, W:]
            real_part = real_part + damping * (src + image_re - real_part)
            imag_part = imag_part + damping * (image_im - imag_part)
            state[...] = jnp.concatenate([real_part, imag_part], axis=1).reshape(state.shape)
        else:
            last[...] = total.reshape(last.shape)
            send(last.at[other_k], last_in, h_sem.at[0, i], h_sem.at[1, i], at(k=other_k))
            arrive(last_in, h_sem.at[0, i], h_sem.at[1, i])
            image = scale16 * (last[my_k] + last_in[...])
            mine = state[my_k]
            out_re[...] = mine[:, :W] + damping * (src16 + image[:, :W] - mine[:, :W])
            out_im[...] = mine[:, W:] + damping * (image[:, W:] - mine[:, W:])

    for copy in sent:
        copy.wait_send()
    gather_close(grid1, 0)
    gather_close(grid2, 1)


def shards(ny, rho_re, rho_im, coulomb, chi_prev, source, band_v, band_c, energy, occ):
    n_pairs = rho_re.shape[1]
    groups, rows, block = chi_prev.shape[1], chi_prev.shape[3], chi_prev.shape[4]
    n_tiles = 2 * (n_pairs // NC // NX // 8)
    per_y = n_tiles // ny
    n = ITERS
    dma = pltpu.SemaphoreType.DMA
    vmem = pltpu.VMEM
    out = jax.ShapeDtypeStruct((rows, W), F32)
    in_vmem = pl.BlockSpec(memory_space=pltpu.VMEM)
    scratch = [
        vmem(chi_prev.shape, F32),
        vmem((2 * block, 16 * groups), BF16),
        vmem((2 * block, 16 * groups), BF16),
        vmem((n_pairs, 192), BF16),
        vmem((64, n_pairs), BF16),
        vmem((64, n_pairs), BF16),
        vmem((2, 16, 2 * W), F32),
        vmem((NC, NX, NZ, 16, W), F32),
        vmem((NC, NX, NZ, 16, 2 * W), F32),
        vmem((n, NC, NX, n_tiles, 8, W), F32),
        vmem((n, NX, n_tiles, 8, W), F32),
        vmem((n, NX, n_tiles, 8, W), F32),
        vmem((n, NX, n_tiles, 8, W), F32),
        vmem((n, ny, per_y, 8, W), F32),
        vmem((n, ny, per_y, 8, W), F32),
        vmem((n, NZ, per_y, 8, W), F32),
        vmem((n, NC, NX, n_tiles, 8, W), F32),
        vmem((n, ny, 32, 2 * W), F32),
        vmem((n, ny, 32, 2 * W), F32),
        vmem((2, 32, 2 * W), F32),
        vmem((2, 16, 2 * W), F32),
        vmem((2, 16, 2 * W), F32),
        vmem((2, 16, 2 * W), F32),
        vmem((16, 2 * W), F32),
        dma(()), dma((2,)),
        dma((n, NZ - 1)), dma((n, NX - 1, NZ)), dma((n, NX)), dma((n, NX, NZ)), dma((n, NX)),
        dma((2, n)), dma((n, NX - 1)), dma((n, NX)), dma((n, ny - 1)), dma((n, ny)),
        dma((n, NZ - 1)), dma((n, NZ)), dma((n, ny - 1)), dma((n, ny)),
        dma((n, NX - 1)), dma((n, NX)), dma((n, NX)), dma((n, NX)),
        dma((n, ny - 1)), dma((n, ny)), dma((2, n)),
    ]
    return pl.pallas_call(
        functools.partial(kernel, ny),
        out_shape=(out, out),
        in_specs=[in_vmem] * 3 + [pl.BlockSpec(memory_space=pl.ANY)] + [in_vmem] * 5,
        out_specs=(in_vmem, in_vmem),
        scratch_shapes=scratch,
        compiler_params=pltpu.CompilerParams(
            collective_id=0, has_side_effects=True, vmem_limit_bytes=48 * 1024 * 1024
        ),
        name="dyson",
    )(
        rho_re, rho_im, coulomb.reshape(1, -1), chi_prev, source,
        band_v.reshape(1, -1), band_c.reshape(1, -1), energy.reshape(1, -1), occ.reshape(1, -1),
    )


def solution(mesh):
    placed = (
        P(("grp", "col"), "dev"),
        P(("grp", "col"), "dev"),
        P(("grp", "col", "dev")),
        P(None, None, "col", "dev", "grp"),
        P(("grp", "col", "dev"), None),
        P("dev"),
        P("dev"),
        P(),
        P(),
    )
    return jax.shard_map(
        functools.partial(shards, mesh.shape["col"]),
        mesh=mesh,
        in_specs=placed,
        out_specs=(P(("grp", "col", "dev"), None), P(("grp", "col", "dev"), None)),
        check_vma=False,
    )
```

time: 815 us -> 105 us (0.13)
  waiting for transfers between devices: 556 us -> 0 us
  blocking collectives: 200 us -> 0 us
  Pallas kernels: 0 us -> 96.2 us
  matrix products: 19.1 us -> 0 us
  between operations: 14 us -> 0.66 us
    reduce_scatter x2 -> x0, waiting for transfers between devices: 458 us -> none  [shards(): lax.psum_scatter(total, ('col', 'dev'), scatter_dimension=0, tiled=True)]
    all_gather x2 -> x0, blocking collectives: 175 us -> none  [shards(): accumulate_piece = lax.all_gather(scaled, 'grp', axis=0, tiled=True)]
    all_gather x2 -> x0, waiting for transfers between devices: 97.1 us -> none  [the longest x1 94.1 us: shards(): piece = lax.all_gather(mine_pairs, 'grp', axis=0, tiled=True)]
    pallas_call x0 -> x1, Pallas kernels: none -> 96.2 us  [shards(): pl.pallas_call(functools.partial(kernel, ny), out_shape=(out, out), in_sp...]
    all_to_all x1 -> x0, blocking collectives: 24.9 us -> none  [shards(): lax.all_to_all(stacked, 'dev', split_axis=0, concat_axis=2, tiled=True)]
    dot_general x6 -> x0, matrix products: 19.1 us -> none  [the longest x2 11.7 us: contract_last(): lax.dot_general(left, right, (((1,), (1,)), ((), ())), precision=lax.Prec...]
  transfers between devices with their start and end apart: 5 -> 0, of which waited for: 4 -> 0; matrix products, arithmetic and copies ran while one was open for 1% -> 0% of each run, Pallas kernels for 0% -> 0%
where the time goes in v1:
time: 105 us
  Pallas kernels  96.2 us (92%)
  local copies, waits for them, and re-layouts  8.18 us (8%)
    pallas_call x1, Pallas kernels, shards(): pl.pallas_call(functools.partial(kernel, ny), out_shape=(out, out), in_sp...  96.2 us
    unnamed x20, local copies, waits for them, and re-layouts  8.18 us

profile of v1, /device:TPU:1, one launch (start us, length us, event | category | flops | bytes accessed | tf_op | source)
XLA Modules:
  0.0 105.0 jit_solution(13110262970834239830)
XLA Ops:
  0.6 0.0 copy-start
  0.6 1.4 %copy-done = f32[2,48,1,16,256]{4,3,2,1,0:T(8,128)S(1)} copy-done((f32[2,48,1,16,256]{4,3,2,1,0:T(8,128)S(1)}, f32[2,48,1,16,256]{4,3,2,1,0:T(8,128)}, u32[]{:S(2)}) %copy-start) | copy-done | bytes 1572888
  2.0 0.0 copy-start.1
  2.0 0.8 copy-done.1
  2.8 0.0 copy-start.2
  2.8 0.8 copy-done.2
  3.6 0.0 copy-start.3
  3.6 0.7 copy-done.3
  4.3 0.0 copy-start.4
  4.3 0.7 copy-done.4
  4.9 0.0 copy-start.5
  4.9 0.7 copy-done.5
  5.6 0.0 copy-start.6
  5.6 0.7 copy-done.6
  6.3 0.0 copy-start.7
  6.3 0.7 copy-done.7
  7.0 0.0 copy-start.8
  7.0 0.7 copy-done.8
  7.6 96.2 %dyson.1 = (f32[16,128]{1,0:T(8,128)S(1)}, f32[16,128]{1,0:T(8,128)S(1)}) custom-call(f32[32,256]{1,0:T(8,128)S(1)} %copy-done.1, f32[32,256]{1,0:T(8,128)S(1)} %copy-done.2, f32[1,16]{1,0:T(1,128)S(1)} %bitcast.9, f32[2,48,1,16,256]{4,3,2,1,0:T(8,128)S(1)} %copy-done, f32[16,128]{1,0:T(8,128)S(1)} %copy-done.3, s32[1,256]{1,0:T(1,128)S(1)} %bitcast.5, ...), custom_call_target="tpu_custom_call" | custom-call | tf_op jit(solution)/shard_map/dyson/pallas_call | solution.py:382
  103.8 0.6 copy.13
  104.5 0.6 copy.14
Async XLA Ops:
  0.6 1.4 %copy-start = (f32[2,48,1,16,256]{4,3,2,1,0:T(8,128)S(1)}, f32[2,48,1,16,256]{4,3,2,1,0:T(8,128)}, u32[]{:S(2)}) copy-start(f32[2,48,1,16,256]{4,3,2,1,0:T(8,128)} %chi_prev.1) | copy-start | bytes 4718596
  2.0 0.8 copy-start.1
  2.8 0.8 copy-start.2
  3.6 0.7 copy-start.3
  4.3 0.7 copy-start.4
  4.9 0.7 copy-start.5
  5.6 0.7 copy-start.6
  6.3 0.7 copy-start.7
  7.0 0.7 copy-start.8

commit v2 on v1

--- a/solution.py
+++ b/solution.py
@@ -36,11 +36,12 @@
     return jnp.sum(jnp.where(down == across, row, 0.0), axis=1, keepdims=True)
 
 
-def kernel(ny, rho_re, rho_im, coulomb, chi_prev, source, band_v, band_c, energy, occ,
-           out_re, out_im,
+def kernel(ny, rho_re_hbm, rho_im_hbm, coulomb_hbm, chi_prev, source_hbm, band_v_hbm, band_c_hbm, energy_hbm, occ_hbm,
+           out,
+           dens, coulomb, source, band_v, band_c, energy, occ, in_sem,
            tile, wide_hi, wide_lo, pairs_t, pairs_w_hi, pairs_w_lo, both, grid1, grid2,
            part0, sib_in, part1, x_in, part2, y_in, z_all, full, sums, sums_in, halves, scaled, state, last, last_in,
-           tile_sem, both_sem, gz_send, gx_send, gs_send, g_recv, gs_recv,
+           both_sem, gz_send, gx_send, gs_send, g_recv, gs_recv,
            sib_sem, xr_send, xr_recv, yr_send, yr_recv, za_send, za_recv, yg_send, yg_recv,
            xg_send, xg_recv, sg_send, sg_recv, rs_send, rs_recv, h_sem):
     grp = lax.axis_index("grp")
@@ -52,7 +53,7 @@
     other_c = 1 - my_c
     other_k = 1 - my_k
     groups = NX * NZ * NC
-    n_pairs = rho_re.shape[1]
+    n_pairs = dens.shape[1]
     n_tiles = full.shape[3]
     per_y = n_tiles // ny
     block = tile.shape[4]
@@ -90,17 +91,28 @@
     def arrive(dst, s, r):
         remote(dst, dst, s, r, at(c=other_c)).wait_recv()
 
-    load = pltpu.make_async_copy(chi_prev, tile, tile_sem)
-    load.start()
+    loads = [
+        pltpu.make_async_copy(src, dst, in_sem.at[j])
+        for j, (src, dst) in enumerate([
+            (coulomb_hbm, coulomb), (source_hbm, source),
+            (band_v_hbm, band_v), (band_c_hbm, band_c), (energy_hbm, energy), (occ_hbm, occ),
+            (rho_re_hbm, dens.at[pl.ds(0, 32)]), (rho_im_hbm, dens.at[pl.ds(32, 32)]),
+            (chi_prev, tile),
+        ])
+    ]
+    for load in loads:
+        load.start()
+    barrier = pltpu.get_barrier_semaphore()
+    for device in everyone:
+        pl.semaphore_signal(barrier, inc=1, device_id=device, device_id_type=MESH)
+    for load in loads[:2]:
+        load.wait()
 
     scale16 = column(coulomb[...])
     src16 = source[...]
     both[my_k] = jnp.concatenate([src16, jnp.broadcast_to(scale16, (16, W))], axis=1)
     grid1[my_c, my_x, my_z] = scale16 * src16
 
-    barrier = pltpu.get_barrier_semaphore()
-    for device in everyone:
-        pl.semaphore_signal(barrier, inc=1, device_id=device, device_id_type=MESH)
     pl.semaphore_wait(barrier, len(everyone))
 
     send(both.at[my_k], both.at[my_k], both_sem.at[0], both_sem.at[1], at(k=other_k))
@@ -232,9 +244,11 @@
         value = dot(left, high) + dot(left, low) + dot(pairs_w_lo[...], high)
         return value[:32, :W] - value[32:, W:], value[:32, W:] + value[32:, :W]
 
-    def scatter_start(re, im, i):
+    def scatter_store(re, im, i):
         for y in range(ny):
             sums[i, y] = jnp.concatenate([re[y * 32 : y * 32 + 32], im[y * 32 : y * 32 + 32]], axis=1)
+
+    def scatter_start(i):
         for j, y in enumerate(y_peers):
             send(sums.at[i, y], sums_in.at[i, my_y], rs_send.at[i, j], rs_recv.at[i, my_y], at(y=y))
 
@@ -247,6 +261,8 @@
 
     gather_start(grid1, 0)
 
+    for load in loads[2:8]:
+        load.wait()
     down = lax.broadcasted_iota(jnp.int32, (energy.shape[1], n_pairs), 0)
     in_v = down == band_v[...]
     in_c = down == band_c[...]
@@ -259,7 +275,7 @@
     delta = pick(in_c, e_col) - pick(in_v, e_col)
     filling = pick(in_v, o_col) - pick(in_c, o_col)
     weight = filling * 2.0 * delta / (delta * delta + frequency * frequency)
-    stacked_pairs = jnp.concatenate([rho_re[...], rho_im[...]], axis=0)
+    stacked_pairs = dens[...]
     high, low = split(stacked_pairs)
     high, low = high.astype(F32), low.astype(F32)
     pairs_t[...] = jnp.concatenate([high, low, high], axis=0).T.astype(BF16)
@@ -267,7 +283,7 @@
     pairs_w_hi[...] = high
     pairs_w_lo[...] = low
 
-    load.wait()
+    loads[8].wait()
     for part in range(2):
         for step in range(groups // 8):
             turned = tile[part, step * 8 : step * 8 + 8, 0].reshape(128, block).T
@@ -277,6 +293,7 @@
             wide_hi[rows, lanes] = high
             wide_lo[rows, lanes] = low
 
+    gather_z(grid1, 0)
     arrive(both.at[other_k], both_sem.at[0], both_sem.at[1])
     held = both[...].reshape(32, 2 * W)
     src = held[:, :W]
@@ -288,25 +305,33 @@
         grid = grid1 if i == 0 else grid2
         v_re = scale * real_part
         v_im = scale * imag_part
-        if i > 0:
+        if i == 0:
+            project(v_re, v_im, i)
+            gather_x(grid, i)
+            reduce_x(i)
+            high, low = gather_end(grid, i)
+            value = dot(wide_hi[...], jnp.concatenate([high, low], axis=1))
+            value = value[:, :W] + value[:, W:] + dot(wide_lo[...], high)
+            scatter_store(value[:block], value[block:], i)
+            reduce_y(i)
+            scatter_start(i)
+            reduce_z(i)
+            spread_y(i)
+        else:
             scaled[...] = jnp.concatenate([v_re, v_im], axis=1).reshape(scaled.shape)
             grid[my_c, my_x, my_z] = scaled[my_k]
             gather_start(grid, i)
-        project(v_re, v_im, i)
-        gather_z(grid, i)
-        reduce_x(i)
-        reduce_y(i)
-        gather_x(grid, i)
-        reduce_z(i)
-        high, low = gather_end(grid, i)
-        if i == 0:
-            value = dot(wide_hi[...], jnp.concatenate([high, low], axis=1))
-            value = value[:, :W] + value[:, W:] + dot(wide_lo[...], high)
-            scatter_start(value[:block], value[block:], i)
-        else:
+            project(v_re, v_im, i)
+            reduce_x(i)
+            gather_z(grid, i)
+            reduce_y(i)
+            gather_x(grid, i)
+            reduce_z(i)
+            high, low = gather_end(grid, i)
             value = dot(wide_hi[...], high) + dot(wide_hi[...], low) + dot(wide_lo[...], high)
-            scatter_start(value[:block, :W] - value[block:, W:], value[:block, W:] + value[block:, :W], i)
-        spread_y(i)
+            scatter_store(value[:block, :W] - value[block:, W:], value[:block, W:] + value[block:, :W], i)
+            spread_y(i)
+            scatter_start(i)
         spread_x(i)
         total = scatter_end(i)
         spread_core(i)
@@ -325,16 +350,15 @@
         else:
             last[...] = total.reshape(last.shape)
             send(last.at[other_k], last_in, h_sem.at[0, i], h_sem.at[1, i], at(k=other_k))
+            for copy in sent:
+                copy.wait_send()
+            gather_close(grid1, 0)
+            gather_close(grid2, 1)
             arrive(last_in, h_sem.at[0, i], h_sem.at[1, i])
             image = scale16 * (last[my_k] + last_in[...])
             mine = state[my_k]
-            out_re[...] = mine[:, :W] + damping * (src16 + image[:, :W] - mine[:, :W])
-            out_im[...] = mine[:, W:] + damping * (image[:, W:] - mine[:, W:])
-
-    for copy in sent:
-        copy.wait_send()
-    gather_close(grid1, 0)
-    gather_close(grid2, 1)
+            out[0] = mine[:, :W] + damping * (src16 + image[:, :W] - mine[:, :W])
+            out[1] = mine[:, W:] + damping * (image[:, W:] - mine[:, W:])
 
 
 def shards(ny, rho_re, rho_im, coulomb, chi_prev, source, band_v, band_c, energy, occ):
@@ -345,9 +369,12 @@
     n = ITERS
     dma = pltpu.SemaphoreType.DMA
     vmem = pltpu.VMEM
-    out = jax.ShapeDtypeStruct((rows, W), F32)
+    out = jax.ShapeDtypeStruct((2, rows, W), F32)
     in_vmem = pl.BlockSpec(memory_space=pltpu.VMEM)
     scratch = [
+        vmem((64, n_pairs), F32), vmem((1, 16), F32), vmem((rows, W), F32),
+        vmem((1, n_pairs), jnp.int32), vmem((1, n_pairs), jnp.int32),
+        vmem((1, energy.shape[0]), F32), vmem((1, energy.shape[0]), F32), dma((9,)),
         vmem(chi_prev.shape, F32),
         vmem((2 * block, 16 * groups), BF16),
         vmem((2 * block, 16 * groups), BF16),
@@ -372,27 +399,33 @@
         vmem((2, 16, 2 * W), F32),
         vmem((2, 16, 2 * W), F32),
         vmem((16, 2 * W), F32),
-        dma(()), dma((2,)),
+        dma((2,)),
         dma((n, NZ - 1)), dma((n, NX - 1, NZ)), dma((n, NX)), dma((n, NX, NZ)), dma((n, NX)),
         dma((2, n)), dma((n, NX - 1)), dma((n, NX)), dma((n, ny - 1)), dma((n, ny)),
         dma((n, NZ - 1)), dma((n, NZ)), dma((n, ny - 1)), dma((n, ny)),
         dma((n, NX - 1)), dma((n, NX)), dma((n, NX)), dma((n, NX)),
         dma((n, ny - 1)), dma((n, ny)), dma((2, n)),
     ]
-    return pl.pallas_call(
+    result = pl.pallas_call(
         functools.partial(kernel, ny),
-        out_shape=(out, out),
-        in_specs=[in_vmem] * 3 + [pl.BlockSpec(memory_space=pl.ANY)] + [in_vmem] * 5,
-        out_specs=(in_vmem, in_vmem),
+        out_shape=out,
+        in_specs=[pl.BlockSpec(memory_space=pltpu.HBM)] * 9,
+        out_specs=in_vmem,
         scratch_shapes=scratch,
         compiler_params=pltpu.CompilerParams(
             collective_id=0, has_side_effects=True, vmem_limit_bytes=48 * 1024 * 1024
         ),
         name="dyson",
     )(
-        rho_re, rho_im, coulomb.reshape(1, -1), chi_prev, source,
-        band_v.reshape(1, -1), band_c.reshape(1, -1), energy.reshape(1, -1), occ.reshape(1, -1),
+        *[
+            pltpu.with_memory_space_constraint(operand, pltpu.HBM)
+            for operand in (
+                rho_re, rho_im, coulomb.reshape(1, -1), chi_prev, source,
+                band_v.reshape(1, -1), band_c.reshape(1, -1), energy.reshape(1, -1), occ.reshape(1, -1),
+            )
+        ]
     )
+    return result[0], result[1]
 
 
 def solution(mesh):

time: 105 us -> 95.2 us (0.907)
  local copies, waits for them, and re-layouts: 8.18 us -> 0.61 us
  Pallas kernels: 96.2 us -> 93.8 us
    unnamed x20 -> x0, local copies, waits for them, and re-layouts: 8.18 us -> none
    pallas_call x1, Pallas kernels: 96.2 us -> 93.8 us  [shards(): pl.pallas_call(functools.partial(kernel, ny), out_shape=out, in_specs=[pl...]
where the time goes in v2:
time: 95.2 us; the launch traced here: 95 us
  Pallas kernels  93.8 us (99%)
    pallas_call x1, Pallas kernels, shards(): pl.pallas_call(functools.partial(kernel, ny), out_shape=out, in_specs=[pl...  93.8 us

profile of v2, /device:TPU:1, one launch (start us, length us, event | category | flops | bytes accessed | tf_op | source)
XLA Modules:
  0.0 95.0 jit_solution(11469984562671595131)
XLA Ops:
  0.6 93.8 %dyson.1 = f32[2,16,128]{2,1,0:T(8,128)S(1)} custom-call(f32[32,256]{1,0:T(8,128)} %rho_re_hbm.1, f32[32,256]{1,0:T(8,128)} %rho_im_hbm.1, f32[1,16]{1,0:T(1,128)} %bitcast.13, f32[2,48,1,16,256]{4,3,2,1,0:T(8,128)} %chi_prev.1, f32[16,128]{1,0:T(8,128)} %source_hbm.1, s32[1,256]{1,0:T(1,128)} %bitcast.9, s32[1,256]{1,0:T(1,128)} %bitcast.10, ...), custom_call_target="tpu_custom_call" | custom-call | tf_op jit(solution)/shard_map/dyson/pallas_call | solution.py:409
  94.4 0.6 slice_bitcast_fusion

commit v3 on v2

--- a/solution.py
+++ b/solution.py
@@ -39,10 +39,10 @@
 def kernel(ny, rho_re_hbm, rho_im_hbm, coulomb_hbm, chi_prev, source_hbm, band_v_hbm, band_c_hbm, energy_hbm, occ_hbm,
            out,
            dens, coulomb, source, band_v, band_c, energy, occ, in_sem,
-           tile, wide_hi, wide_lo, pairs_t, pairs_w_hi, pairs_w_lo, both, grid1, grid2,
-           part0, sib_in, part1, x_in, part2, y_in, z_all, full, sums, sums_in, halves, scaled, state, last, last_in,
-           both_sem, gz_send, gx_send, gs_send, g_recv, gs_recv,
-           sib_sem, xr_send, xr_recv, yr_send, yr_recv, za_send, za_recv, yg_send, yg_recv,
+           tile, wide_hi, wide_lo, pairs_t, pairs_w, both, grid1, grid2,
+           part0, sib_in, part1, x_in, part2, y_in, z_all, full, sums, sums_in, halves, scaled, state, last, last_in, product,
+           both_sem, w_sem, gz_send, gx_send, gs_send, g_recv, gs_recv,
+           sib_send, sib_recv, xr_send, xr_recv, yr_send, yr_recv, za_send, za_recv, yg_send, yg_recv,
            xg_send, xg_recv, sg_send, sg_recv, rs_send, rs_recv, h_sem):
     grp = lax.axis_index("grp")
     my_y = lax.axis_index("col")
@@ -68,11 +68,14 @@
 
     x_peers = [lax.rem(my_x + d, NX) for d in range(1, NX)]
     y_peers = [lax.rem(my_y + d, ny) for d in range(1, ny)]
+    x_order = x_peers[1:2] + x_peers[:1] + x_peers[2:] + [my_x]
     z_peers = [lax.rem(my_z + d, NZ) for d in range(1, NZ)]
+    ring = [(my_z, other_k)] + [(z, k) for z in z_peers for k in (other_k, my_k)]
     everyone = (
         [at(x=x) for x in x_peers]
         + [at(y=y) for y in y_peers]
         + [at(z=z) for z in z_peers]
+        + [at(z=z, k=other_k) for z in z_peers]
         + [at(c=other_c), at(k=other_k)]
     )
 
@@ -179,12 +182,15 @@
                     row = (c * NX + x) * count + (t // 2) * 8
                     lane = (t % 2) * W
                     part0[i, c, x, t] = value[row : row + 8, lane : lane + W]
-        send(part0.at[i, other_c], sib_in.at[i], sib_sem.at[0, i], sib_sem.at[1, i], at(c=other_c))
+        for x in x_order:
+            send(part0.at[i, other_c, x], sib_in.at[i, x], sib_send.at[i, x], sib_recv.at[i, x], at(c=other_c))
 
     def reduce_x(i):
-        arrive(sib_in.at[i], sib_sem.at[0, i], sib_sem.at[1, i])
-        part1[i] = part0[i, my_c] + sib_in[i]
-        for j, x in enumerate(x_peers):
+        for j, x in enumerate(x_order):
+            arrive(sib_in.at[i, x], sib_send.at[i, x], sib_recv.at[i, x])
+            part1[i, x] = part0[i, my_c, x] + sib_in[i, x]
+            if j == NX - 1:
+                continue
             send(part1.at[i, x], x_in.at[i, my_x], xr_send.at[i, j], xr_recv.at[i, my_x], at(x=x))
 
     def reduce_y(i):
@@ -201,19 +207,21 @@
         for y in y_peers:
             arrive(y_in.at[i, y], yr_send.at[i, 0], yr_recv.at[i, y])
             total = total + y_in[i, y]
-        z_all[i, my_z] = total
-        for j, z in enumerate(z_peers):
-            send(z_all.at[i, my_z], z_all.at[i, my_z], za_send.at[i, j], za_recv.at[i, my_z], at(z=z))
+        z_all[i, my_k, my_z] = total
+        own = z_all.at[i, my_k, my_z]
+        for j, (z, k) in enumerate(ring):
+            send(own, own, za_send.at[i, j], za_recv.at[i, my_k, my_z], at(z=z, k=k))
 
     def spread_y(i):
-        for z in z_peers:
-            arrive(z_all.at[i, z], za_send.at[i, 0], za_recv.at[i, z])
-        total = z_all[i, 0]
-        for z in range(1, NZ):
-            total = total + z_all[i, z]
-        mine = pl.ds(my_y * per_y, per_y)
-        full[i, my_c, my_x, mine] = total
-        own = full.at[i, my_c, my_x, mine]
+        for z, k in ring:
+            arrive(z_all.at[i, k, z], za_send.at[i, 0], za_recv.at[i, k, z])
+        for k in range(2):
+            total = z_all[i, k, 0]
+            for z in range(1, NZ):
+                total = total + z_all[i, k, z]
+            for t in range(per_y):
+                full[i, my_c, my_x, my_y * per_y + t, k] = total[t]
+        own = full.at[i, my_c, my_x, pl.ds(my_y * per_y, per_y)]
         for j, y in enumerate(y_peers):
             send(own, own, yg_send.at[i, j], yg_recv.at[i, my_y], at(y=y))
 
@@ -237,12 +245,15 @@
         lanes = []
         for lane in range(2):
             lanes.append(jnp.concatenate(
-                [full[i, c, x, t] for c in range(NC) for x in range(NX) for t in range(lane, n_tiles, 2)], axis=0
+                [full[i, c, x, t, k]
+                 for k in range(2) for c in range(NC) for x in range(NX) for t in range(lane, n_tiles, 2)], axis=0
             ))
         high, low = split(jnp.concatenate(lanes, axis=1))
-        left = pairs_w_hi[...]
-        value = dot(left, high) + dot(left, low) + dot(pairs_w_lo[...], high)
-        return value[:32, :W] - value[32:, W:], value[:32, W:] + value[32:, :W]
+        left_hi, left_lo = split(jnp.concatenate([pairs_w[0], pairs_w[1]], axis=1))
+        value = dot(left_hi, high) + dot(left_hi, low) + dot(left_lo, high)
+        return jnp.concatenate(
+            [value[:32, :W] - value[32:, W:], value[:32, W:] + value[32:, :W]], axis=1
+        )
 
     def scatter_store(re, im, i):
         for y in range(ny):
@@ -279,9 +290,7 @@
     high, low = split(stacked_pairs)
     high, low = high.astype(F32), low.astype(F32)
     pairs_t[...] = jnp.concatenate([high, low, high], axis=0).T.astype(BF16)
-    high, low = split(stacked_pairs * weight)
-    pairs_w_hi[...] = high
-    pairs_w_lo[...] = low
+    pairs_w[my_k] = stacked_pairs * weight
 
     loads[8].wait()
     for part in range(2):
@@ -309,6 +318,7 @@
             project(v_re, v_im, i)
             gather_x(grid, i)
             reduce_x(i)
+            send(pairs_w.at[my_k], pairs_w.at[my_k], w_sem.at[0], w_sem.at[1], at(k=other_k))
             high, low = gather_end(grid, i)
             value = dot(wide_hi[...], jnp.concatenate([high, low], axis=1))
             value = value[:, :W] + value[:, W:] + dot(wide_lo[...], high)
@@ -316,7 +326,6 @@
             reduce_y(i)
             scatter_start(i)
             reduce_z(i)
-            spread_y(i)
         else:
             scaled[...] = jnp.concatenate([v_re, v_im], axis=1).reshape(scaled.shape)
             grid[my_c, my_x, my_z] = scaled[my_k]
@@ -330,32 +339,31 @@
             high, low = gather_end(grid, i)
             value = dot(wide_hi[...], high) + dot(wide_hi[...], low) + dot(wide_lo[...], high)
             scatter_store(value[:block, :W] - value[block:, W:], value[:block, W:] + value[block:, :W], i)
-            spread_y(i)
             scatter_start(i)
-        spread_x(i)
-        total = scatter_end(i)
-        spread_core(i)
-        q_re, q_im = expand(i)
-        total = total - jnp.concatenate([q_re, q_im], axis=1)
+        spread_y(i)
         if i < ITERS - 1:
-            halves[my_k] = total
+            halves[my_k] = scatter_end(i)
             send(halves.at[my_k], halves.at[my_k], h_sem.at[0, i], h_sem.at[1, i], at(k=other_k))
+            spread_x(i)
+            spread_core(i)
             arrive(halves.at[other_k], h_sem.at[0, i], h_sem.at[1, i])
-            image = halves[0] + halves[1]
-            image_re = scale * image[:, :W]
-            image_im = scale * image[:, W:]
-            real_part = real_part + damping * (src + image_re - real_part)
-            imag_part = imag_part + damping * (image_im - imag_part)
+            arrive(pairs_w.at[other_k], w_sem.at[0], w_sem.at[1])
+            image = halves[0] + halves[1] - expand(i)
+            real_part = real_part + damping * (src + scale * image[:, :W] - real_part)
+            imag_part = imag_part + damping * (scale * image[:, W:] - imag_part)
             state[...] = jnp.concatenate([real_part, imag_part], axis=1).reshape(state.shape)
         else:
-            last[...] = total.reshape(last.shape)
+            last[...] = scatter_end(i).reshape(last.shape)
             send(last.at[other_k], last_in, h_sem.at[0, i], h_sem.at[1, i], at(k=other_k))
+            spread_x(i)
+            spread_core(i)
             for copy in sent:
                 copy.wait_send()
             gather_close(grid1, 0)
             gather_close(grid2, 1)
             arrive(last_in, h_sem.at[0, i], h_sem.at[1, i])
-            image = scale16 * (last[my_k] + last_in[...])
+            product[...] = expand(i).reshape(product.shape)
+            image = scale16 * (last[my_k] + last_in[...] - product[my_k])
             mine = state[my_k]
             out[0] = mine[:, :W] + damping * (src16 + image[:, :W] - mine[:, :W])
             out[1] = mine[:, W:] + damping * (image[:, W:] - mine[:, W:])
@@ -379,8 +387,7 @@
         vmem((2 * block, 16 * groups), BF16),
         vmem((2 * block, 16 * groups), BF16),
         vmem((n_pairs, 192), BF16),
-        vmem((64, n_pairs), BF16),
-        vmem((64, n_pairs), BF16),
+        vmem((2, 64, n_pairs), F32),
         vmem((2, 16, 2 * W), F32),
         vmem((NC, NX, NZ, 16, W), F32),
         vmem((NC, NX, NZ, 16, 2 * W), F32),
@@ -390,8 +397,8 @@
         vmem((n, NX, n_tiles, 8, W), F32),
         vmem((n, ny, per_y, 8, W), F32),
         vmem((n, ny, per_y, 8, W), F32),
-        vmem((n, NZ, per_y, 8, W), F32),
-        vmem((n, NC, NX, n_tiles, 8, W), F32),
+        vmem((n, 2, NZ, per_y, 8, W), F32),
+        vmem((n, NC, NX, n_tiles, 2, 8, W), F32),
         vmem((n, ny, 32, 2 * W), F32),
         vmem((n, ny, 32, 2 * W), F32),
         vmem((2, 32, 2 * W), F32),
@@ -399,10 +406,11 @@
         vmem((2, 16, 2 * W), F32),
         vmem((2, 16, 2 * W), F32),
         vmem((16, 2 * W), F32),
-        dma((2,)),
+        vmem((2, 16, 2 * W), F32),
+        dma((2,)), dma((2,)),
         dma((n, NZ - 1)), dma((n, NX - 1, NZ)), dma((n, NX)), dma((n, NX, NZ)), dma((n, NX)),
-        dma((2, n)), dma((n, NX - 1)), dma((n, NX)), dma((n, ny - 1)), dma((n, ny)),
-        dma((n, NZ - 1)), dma((n, NZ)), dma((n, ny - 1)), dma((n, ny)),
+        dma((n, NX)), dma((n, NX)), dma((n, NX - 1)), dma((n, NX)), dma((n, ny - 1)), dma((n, ny)),
+        dma((n, 2 * NZ - 1)), dma((n, 2, NZ)), dma((n, ny - 1)), dma((n, ny)),
         dma((n, NX - 1)), dma((n, NX)), dma((n, NX)), dma((n, NX)),
         dma((n, ny - 1)), dma((n, ny)), dma((2, n)),
     ]

time: 95.2 us -> 89.1 us (0.936)
  Pallas kernels: 93.8 us -> 87.7 us
    pallas_call x1, Pallas kernels: 93.8 us -> 87.7 us  [shards(): pl.pallas_call(functools.partial(kernel, ny), out_shape=out, in_specs=[pl...]
where the time goes in v3:
time: 89.1 us; the launch traced here: 88.9 us
  Pallas kernels  87.7 us (98%)
    pallas_call x1, Pallas kernels, shards(): pl.pallas_call(functools.partial(kernel, ny), out_shape=out, in_specs=[pl...  87.7 us

profile of v3, /device:TPU:1, one launch (start us, length us, event | category | flops | bytes accessed | tf_op | source)
XLA Modules:
  0.0 88.9 jit_solution(13975895720027904095)
XLA Ops:
  0.6 87.7 %dyson.1 = f32[2,16,128]{2,1,0:T(8,128)S(1)} custom-call(f32[32,256]{1,0:T(8,128)} %rho_re_hbm.1, f32[32,256]{1,0:T(8,128)} %rho_im_hbm.1, f32[1,16]{1,0:T(1,128)} %bitcast.13, f32[2,48,1,16,256]{4,3,2,1,0:T(8,128)} %chi_prev.1, f32[16,128]{1,0:T(8,128)} %source_hbm.1, s32[1,256]{1,0:T(1,128)} %bitcast.9, s32[1,256]{1,0:T(1,128)} %bitcast.10, ...), custom_call_target="tpu_custom_call" | custom-call | tf_op jit(solution)/shard_map/dyson/pallas_call | solution.py:417
  88.3 0.6 slice_bitcast_fusion

commit v4 on v3

--- a/solution.py
+++ b/solution.py
@@ -316,8 +316,8 @@
         v_im = scale * imag_part
         if i == 0:
             project(v_re, v_im, i)
+            reduce_x(i)
             gather_x(grid, i)
-            reduce_x(i)
             send(pairs_w.at[my_k], pairs_w.at[my_k], w_sem.at[0], w_sem.at[1], at(k=other_k))
             high, low = gather_end(grid, i)
             value = dot(wide_hi[...], jnp.concatenate([high, low], axis=1))
@@ -334,8 +334,8 @@
             reduce_x(i)
             gather_z(grid, i)
             reduce_y(i)
+            reduce_z(i)
             gather_x(grid, i)
-            reduce_z(i)
             high, low = gather_end(grid, i)
             value = dot(wide_hi[...], high) + dot(wide_hi[...], low) + dot(wide_lo[...], high)
             scatter_store(value[:block, :W] - value[block:, W:], value[:block, W:] + value[block:, :W], i)

time: 89.1 us -> 86.3 us (0.969)
  Pallas kernels: 87.7 us -> 84.9 us
    pallas_call x1, Pallas kernels: 87.7 us -> 84.9 us  [shards(): pl.pallas_call(functools.partial(kernel, ny), out_shape=out, in_specs=[pl...]
where the time goes in v4:
time: 86.3 us; the launch traced here: 86.2 us
  Pallas kernels  84.9 us (98%)
    pallas_call x1, Pallas kernels, shards(): pl.pallas_call(functools.partial(kernel, ny), out_shape=out, in_specs=[pl...  84.9 us

profile of v4, /device:TPU:1, one launch (start us, length us, event | category | flops | bytes accessed | tf_op | source)
XLA Modules:
  0.0 86.2 jit_solution(16536165379976187098)
XLA Ops:
  0.6 84.9 %dyson.1 = f32[2,16,128]{2,1,0:T(8,128)S(1)} custom-call(f32[32,256]{1,0:T(8,128)} %rho_re_hbm.1, f32[32,256]{1,0:T(8,128)} %rho_im_hbm.1, f32[1,16]{1,0:T(1,128)} %bitcast.13, f32[2,48,1,16,256]{4,3,2,1,0:T(8,128)} %chi_prev.1, f32[16,128]{1,0:T(8,128)} %source_hbm.1, s32[1,256]{1,0:T(1,128)} %bitcast.9, s32[1,256]{1,0:T(1,128)} %bitcast.10, ...), custom_call_target="tpu_custom_call" | custom-call | tf_op jit(solution)/shard_map/dyson/pallas_call | solution.py:417
  85.6 0.6 slice_bitcast_fusion

commit v5 on v4

--- a/solution.py
+++ b/solution.py
@@ -66,9 +66,9 @@
         k = my_k if k is None else k
         return ((x * NZ + z) * NC + c, y, k)
 
-    x_peers = [lax.rem(my_x + d, NX) for d in range(1, NX)]
-    y_peers = [lax.rem(my_y + d, ny) for d in range(1, ny)]
-    x_order = x_peers[1:2] + x_peers[:1] + x_peers[2:] + [my_x]
+    x_peers = [lax.rem(my_x + d, NX) for d in sorted(range(1, NX), key=lambda d: -min(d, NX - d))]
+    y_peers = [lax.rem(my_y + d, ny) for d in sorted(range(1, ny), key=lambda d: -min(d, ny - d))]
+    x_order = x_peers + [my_x]
     z_peers = [lax.rem(my_z + d, NZ) for d in range(1, NZ)]
     ring = [(my_z, other_k)] + [(z, k) for z in z_peers for k in (other_k, my_k)]
     everyone = (
@@ -147,8 +147,7 @@
         send(row, row, gs_send.at[i, my_x], gs_recv.at[i, my_x], at(c=other_c))
 
     def gather_x(grid, i):
-        for j in (0, NX - 2, 1) if NX == 4 else range(NX - 1):
-            x = x_peers[j]
+        for x in reversed(x_peers):
             for z in range(NZ):
                 arrive(grid.at[my_c, x, z], gz_send.at[i, 0], g_recv.at[i, x, z])
             row = grid.at[my_c, x]
@@ -234,7 +233,7 @@
         send(own, own, sg_send.at[i, my_x], sg_recv.at[i, my_x], at(c=other_c))
 
     def spread_core(i):
-        for x in x_peers:
+        for x in reversed(x_peers):
             held = full.at[i, my_c, x]
             arrive(held, xg_send.at[i, 0], xg_recv.at[i, x])
             send(held, held, sg_send.at[i, x], sg_recv.at[i, x], at(c=other_c))

time: 86.3 us -> 85.1 us (0.986)
  Pallas kernels: 84.9 us -> 83.7 us
    pallas_call x1, Pallas kernels: 84.9 us -> 83.7 us  [shards(): pl.pallas_call(functools.partial(kernel, ny), out_shape=out, in_specs=[pl...]
where the time goes in v5:
time: 85.1 us; the launch traced here: 85 us
  Pallas kernels  83.7 us (98%)
    pallas_call x1, Pallas kernels, shards(): pl.pallas_call(functools.partial(kernel, ny), out_shape=out, in_specs=[pl...  83.7 us

profile of v5, /device:TPU:1, one launch (start us, length us, event | category | flops | bytes accessed | tf_op | source)
XLA Modules:
  0.0 85.0 jit_solution(9997792574679742257)
XLA Ops:
  0.6 83.7 %dyson.1 = f32[2,16,128]{2,1,0:T(8,128)S(1)} custom-call(f32[32,256]{1,0:T(8,128)} %rho_re_hbm.1, f32[32,256]{1,0:T(8,128)} %rho_im_hbm.1, f32[1,16]{1,0:T(1,128)} %bitcast.13, f32[2,48,1,16,256]{4,3,2,1,0:T(8,128)} %chi_prev.1, f32[16,128]{1,0:T(8,128)} %source_hbm.1, s32[1,256]{1,0:T(1,128)} %bitcast.9, s32[1,256]{1,0:T(1,128)} %bitcast.10, ...), custom_call_target="tpu_custom_call" | custom-call | tf_op jit(solution)/shard_map/dyson/pallas_call | solution.py:416
  84.4 0.6 slice_bitcast_fusion
